TPU v7x, 128 devices: a whole 4x4x4 slice. The times are simulated.
128 devices in a mesh: prow: 8 (over y, core), pcol: 16 (over x, z).
Axes of the slice: x: 4, y: 4, z: 4, core: 2. Of those that a mesh axis runs over, the one named last changes fastest.
Arguments:
- cross_cov: float32 [2, 512, 16384], P(None, 'prow', 'pcol'), may hold values from -6 to 6
- prev_rows: bfloat16 [2, 512, 32768], P(None, 'pcol', 'prow'), may hold values from -0.046875 to 0.046875
- prev_solved: bfloat16 [32768, 16384], P('prow', 'pcol'), may hold values from -6 to 6
- sub_block: float32 [512, 512], replicated, may hold values from -0.25 to 0.25
- inv_first: float32 [512, 512], replicated, as said below
- inv_second: float32 [512, 512], replicated, as said below
Outputs:
- solved: float32 [2, 512, 16384], P(None, 'prow', 'pcol')
Inputs may be any that keep to these rules, and one draw needn't show every extreme that they name: inv_first is lower triangular with a positive diagonal. inv_second is lower triangular with a positive diagonal.
All inputs are finite; a program needn't handle non-finite values.
Results may differ from a plain program's by a relative error of at most 0.0003.
Values may be sent and summed in bfloat16 or wider, within the bound.
A program may use at most 64 MiB of HBM per device.

v0:
```python
import jax
import jax.numpy as jnp
from jax import lax
from jax.sharding import PartitionSpec as P


def mult(left, right):
    return jnp.dot(left, right, preferred_element_type=jnp.float32, precision=lax.Precision.HIGH)


def local(cross_cov, prev_rows, prev_solved, sub_block, inv_first, inv_second):
    rows = cross_cov.shape[1]
    terms = jnp.einsum(
        "kra,ac->krc",
        lax.all_gather(prev_rows, "pcol", axis=1, tiled=True),
        prev_solved,
        preferred_element_type=jnp.float32,
    )
    offset = lax.axis_index("prow") * rows
    rhs = lax.dynamic_update_slice_in_dim(
        -terms, lax.dynamic_slice_in_dim(-terms, offset, rows, 1) + cross_cov, offset, 1
    )
    first = mult(inv_first, rhs[0])
    second = mult(inv_second, rhs[1] - mult(sub_block, first))
    both = jnp.concatenate([first, second]).reshape((2,) + first.shape)
    return lax.psum_scatter(both, "prow", scatter_dimension=1, tiled=True)


def solution(mesh):
    return jax.shard_map(
        local,
        mesh=mesh,
        in_specs=(
            P(None, "prow", "pcol"),
            P(None, "pcol", "prow"),
            P("prow", "pcol"),
            P(),
            P(),
            P(),
        ),
        out_specs=P(None, "prow", "pcol"),
        check_vma=False,
    )
```

profile of v0, /device:TPU:0, one launch (start us, length us, event | category | flops | bytes accessed | tf_op | source)
XLA Modules:
  0.0 148.7 jit_solution(808641312518555056)
XLA Ops:
  6.5 0.0 copy-start
  6.5 0.0 all-gather.2.cloned.1.call-start
  6.5 0.7 all-gather.2.cloned.1.call-update
  7.3 0.0 reduce-scatter.2.cloned.1.call-start
  7.3 0.0 copy-start.3
  7.3 75.6 %all-gather.2.cloned.1.call-done = bf16[2,512,4096]{2,1,0:T(8,128)(2,1)} async-done(((bf16[2,32,4096]{2,1,0:T(8,128)(2,1)}), bf16[2,512,4096]{2,1,0:T(8,128)(2,1)}) %all-gather.2.cloned.1.call-update) | async-done | bytes 8388624 | tf_op jit(solution)/shard_map/all_gather | solution.py:15
  82.9 13.1 %fusion.2 = f32[2,512,1024]{2,1,0:T(8,128)S(1)} fusion(bf16[2,512,4096]{2,1,0:T(8,128)(2,1)} %all-gather.2.cloned.1.call-done, bf16[4096,1024]{1,0:T(8,128)(2,1)} %param.8), kind=kOutput, calls=%fused_computation.3 | convolution fusion | flops 8590983168 | bytes 20971520 | tf_op jit(solution)/shard_map/kra,ac->krc/dot_general | solution.py:13
  96.0 0.0 copy-done.3
  96.0 0.0 copy-start.1
  96.0 0.1 add_dynamic-update-slice_fusion
  96.2 0.0 copy-done
  96.2 0.0 copy-start.2
  96.2 1.9 %fusion.8 = f32[1024,512]{0,1:T(8,128)S(1)} fusion(f32[512,512]{1,0:T(8,128)S(1)} %copy-done, f32[2,512,1024]{2,1,0:T(8,128)S(1)} %add_dynamic-update-slice_fusion), kind=kOutput, calls=%fused_computation.8 | convolution fusion | flops 1610612736 | bytes 5242880 | tf_op jit(solution)/shard_map/dot_general | solution.py:8
  98.0 0.0 copy-done.1
  98.1 1.9 %fusion.13 = f32[1024,512]{0,1:T(8,128)S(1)} fusion(f32[1024,512]{0,1:T(8,128)S(1)} %fusion.8, f32[512,512]{1,0:T(8,128)S(1)} %copy-done.1), kind=kOutput, calls=%fused_computation.12 | convolution fusion | flops 1610612736 | bytes 5242880 | tf_op jit(solution)/shard_map/dot_general | solution.py:8
  100.0 0.0 copy-done.2
  100.0 1.9 %fusion.10 = f32[512,1024]{1,0:T(8,128)S(1)} fusion(f32[512,512]{1,0:T(8,128)S(1)} %copy-done.2, f32[2,512,1024]{2,1,0:T(8,128)S(1)} %add_dynamic-update-slice_fusion, f32[1024,512]{0,1:T(8,128)S(1)} %fusion.13), kind=kOutput, calls=%fused_computation.10 | convolution fusion | flops 1611137024 | bytes 7340032 | tf_op jit(solution)/shard_map/dot_general | solution.py:8
  101.9 2.5 %pad_maximum_fusion = f32[1024,1024]{1,0:T(8,128)} fusion(f32[512,1024]{1,0:T(8,128)S(1)} %fusion.10, f32[512,1024]{1,0:T(8,128)S(1)} %bitcast.31), kind=kLoop, calls=%fused_computation.2 | loop fusion | flops 1048576 | bytes 8388608 | tf_op jit(solution)/shard_map/concatenate | solution.py:25
  104.3 0.0 reduce-scatter.2.cloned.1.call-update
  104.4 37.5 %reduce-scatter.2.cloned.1.call-done = f32[2,64,1024]{2,1,0:T(8,128)} async-done(((f32[2,512,1024]{2,1,0:T(8,128)}), f32[2,64,1024]{2,1,0:T(8,128)}) %reduce-scatter.2.cloned.1.call-update) | async-done | bytes 524304 | tf_op jit(solution)/shard_map/reduce_scatter | solution.py:26
Async XLA Ops:
  6.5 89.6 %copy-start = (f32[512,512]{1,0:T(8,128)S(1)}, f32[512,512]{1,0:T(8,128)}, u32[]{:S(2)}) copy-start(f32[512,512]{1,0:T(8,128)} %param.10) | copy-start | bytes 3145732
  6.5 76.4 %all-gather.2.cloned.1.call-start = ((), (), s32[]{:S(2)}) async-start(), calls=%async_computation.1 | async-start | bytes 8912896 | tf_op jit(solution)/shard_map/all_gather | solution.py:15
  7.3 134.6 %reduce-scatter.2.cloned.1.call-start = ((), (), s32[]{:S(2)}) async-start(), calls=%async_computation.2 | async-start | bytes 4718592 | tf_op jit(solution)/shard_map/reduce_scatter | solution.py:26
  7.3 88.7 %copy-start.3 = (f32[2,64,1024]{2,1,0:T(8,128)S(1)}, f32[2,64,1024]{2,1,0:T(8,128)}, u32[]{:S(2)}) copy-start(f32[2,64,1024]{2,1,0:T(8,128)} %param.6) | copy-start | bytes 1572868
  96.0 2.0 %copy-start.1 = (f32[512,512]{1,0:T(8,128)S(1)}, f32[512,512]{1,0:T(8,128)}, u32[]{:S(2)}) copy-start(f32[512,512]{1,0:T(8,128)} %param.9) | copy-start | bytes 3145732
  96.2 3.8 %copy-start.2 = (f32[512,512]{1,0:T(8,128)S(1)}, f32[512,512]{1,0:T(8,128)}, u32[]{:S(2)}) copy-start(f32[512,512]{1,0:T(8,128)} %param.11) | copy-start | bytes 3145732
Sparse Core Ops, SparseCore 0:
  9.6 73.3 all-gather.1
  104.5 37.3 reduce-scatter.1
where the time goes:
time: 149 us
  waiting for transfers between devices  114 us (77%)
  matrix products  18.7 us (13%)
  between operations  13.5 us (9%)
  other arithmetic  2.58 us (2%)
    all_gather x1, waiting for transfers between devices, local(): lax.all_gather(prev_rows, 'pcol', axis=1, tiled=True)  75.6 us
    reduce_scatter x1, waiting for transfers between devices, local(): return lax.psum_scatter(both, 'prow', scatter_dimension=1, tiled=True)  37.5 us
    dot_general x1, matrix products, local(): jnp.einsum('kra,ac->krc', lax.all_gather(prev_rows, 'pcol', axis=1, tiled...  13.1 us
    dot_general x3, matrix products, mult(): jnp.dot(left, right, preferred_element_type=jnp.float32, precision=lax.Pr...  5.64 us
  transfers between devices with their start and end apart: 2, of which 2 were waited for; matrix products, arithmetic and copies ran while one was open for 0% of the time, Pallas kernels for 0%

commit v1 on v0

--- a/solution.py
+++ b/solution.py
@@ -2,6 +2,7 @@
 import jax.numpy as jnp
 from jax import lax
 from jax.sharding import PartitionSpec as P
+from jax.lax import all_to_all, axis_size
 
 
 def mult(left, right):
@@ -12,7 +13,9 @@
     rows = cross_cov.shape[1]
     terms = jnp.einsum(
         "kra,ac->krc",
-        lax.all_gather(prev_rows, "pcol", axis=1, tiled=True),
+        jnp.concatenate(
+            all_to_all(jnp.stack(axis_size("pcol") * [prev_rows]), "pcol", 0, 0), axis=1
+        ),
         prev_solved,
         preferred_element_type=jnp.float32,
     )

time: 149 us -> 245 us (1.64)
  waiting for transfers between devices: 114 us -> 188 us
  local copies, waits for them, and re-layouts: 0.02 us -> 13.2 us
  starting transfers between devices: 0.04 us -> 8.05 us
    all_to_all x0 -> x1, waiting for transfers between devices: none -> 148 us  [local(): all_to_all(jnp.stack(axis_size('pcol') * [prev_rows]), 'pcol', 0, 0)]
    all_gather x1 -> x0, waiting for transfers between devices: 75.6 us -> none  [local(): lax.all_gather(prev_rows, 'pcol', axis=1, tiled=True)]
    all_to_all x0 -> x1, starting transfers between devices: none -> 8.01 us  [local(): all_to_all(jnp.stack(axis_size('pcol') * [prev_rows]), 'pcol', 0, 0)]
    reshape x0 -> x1, local copies, waits for them, and re-layouts: none -> 7.72 us  [local(): jnp.concatenate(all_to_all(jnp.stack(axis_size('pcol') * [prev_rows]), 'p...]
    another operation x0 -> x1, local copies, waits for them, and re-layouts: none -> 5.43 us  [local(): jnp.stack(axis_size('pcol') * [prev_rows])]
    reduce_scatter x1, waiting for transfers between devices: 37.5 us -> 40.8 us  [local(): return lax.psum_scatter(both, 'prow', scatter_dimension=1, tiled=True)]
where the time goes in v1:
time: 245 us
  waiting for transfers between devices  188 us (77%)
  matrix products  18.8 us (8%)
  between operations  13.5 us (6%)
  local copies, waits for them, and re-layouts  13.2 us (5%)
  starting transfers between devices  8.05 us (3%)
  other arithmetic  2.57 us (1%)
    all_to_all x1, waiting for transfers between devices, local(): all_to_all(jnp.stack(axis_size('pcol') * [prev_rows]), 'pcol', 0, 0)  148 us
    reduce_scatter x1, waiting for transfers between devices, local(): return lax.psum_scatter(both, 'prow', scatter_dimension=1, tiled=True)  40.8 us
    dot_general x1, matrix products, local(): jnp.einsum('kra,ac->krc', jnp.concatenate(all_to_all(jnp.stack(axis_size(...  13.1 us
    all_to_all x1, starting transfers between devices, local(): all_to_all(jnp.stack(axis_size('pcol') * [prev_rows]), 'pcol', 0, 0)  8.01 us
    reshape x1, local copies, waits for them, and re-layouts, local(): jnp.concatenate(all_to_all(jnp.stack(axis_size('pcol') * [prev_rows]), 'p...  7.72 us
    dot_general x3, matrix products, mult(): jnp.dot(left, right, preferred_element_type=jnp.float32, precision=lax.Pr...  5.64 us
    another operation x1, local copies, waits for them, and re-layouts, local(): jnp.stack(axis_size('pcol') * [prev_rows])  5.43 us
  transfers between devices with their start and end apart: 2, of which 2 were waited for; matrix products, arithmetic and copies ran while one was open for 0% of the time, Pallas kernels for 0%

profile of v1, /device:TPU:0, one launch (start us, length us, event | category | flops | bytes accessed | tf_op | source)
XLA Modules:
  0.0 244.5 jit_solution(6928259550333994259)
XLA Ops:
  6.5 0.0 copy-start
  6.5 5.4 %stack.2 = bf16[16,2,32,4096]{3,2,1,0:T(8,128)(2,1)} broadcast(bf16[2,32,4096]{2,1,0:T(8,128)(2,1)} %param.7), dimensions={1,2,3} | broadcast | bytes 8912896 | tf_op jit(solution)/shard_map/stack | solution.py:17
  12.0 8.0 %all-to-all-start = ((bf16[16,2,32,4096]{3,2,1,0:T(8,128)(2,1)}), bf16[16,2,32,4096]{3,2,1,0:T(8,128)(2,1)}, u32[]{:S(2)}, u32[]{:S(2)}) async-start(bf16[16,2,32,4096]{3,2,1,0:T(8,128)(2,1)} %stack.2), calls=%async_computation | async-start | bytes 16777216 | tf_op jit(solution)/shard_map/all_to_all | solution.py:17
  20.0 0.0 reduce-scatter.2.cloned.1.call-start
  20.0 147.6 %all-to-all-done = bf16[16,2,32,4096]{3,2,1,0:T(8,128)(2,1)} async-done(((bf16[16,2,32,4096]{3,2,1,0:T(8,128)(2,1)}), bf16[16,2,32,4096]{3,2,1,0:T(8,128)(2,1)}, u32[]{:S(2)}, u32[]{:S(2)}) %all-to-all-start) | async-done | bytes 8388640 | tf_op jit(solution)/shard_map/all_to_all | solution.py:17
  167.7 7.7 %copy.7 = bf16[2,16,32,4096]{3,2,1,0:T(8,128)(2,1)} copy(bf16[2,16,32,4096]{3,2,0,1:T(8,128)(2,1)} %bitcast) | data formatting | bytes 16777216 | tf_op jit(solution)/shard_map/reshape | solution.py:16
  175.4 0.0 copy-start.3
  175.4 13.1 %fusion.2 = f32[2,512,1024]{2,1,0:T(8,128)S(1)} fusion(bf16[2,512,4096]{2,1,0:T(8,128)(2,1)} %bitcast.35, bf16[4096,1024]{1,0:T(8,128)(2,1)} %param.8), kind=kOutput, calls=%fused_computation.3 | convolution fusion | flops 8590983168 | bytes 20971520 | tf_op jit(solution)/shard_map/kra,ac->krc/dot_general | solution.py:14
  188.5 0.0 copy-done.3
  188.5 0.0 copy-start.1
  188.5 0.1 add_dynamic-update-slice_fusion
  188.6 0.0 copy-done
  188.7 0.0 copy-start.2
  188.7 1.9 fusion.8
  190.5 0.0 copy-done.1
  190.5 1.9 fusion.13
  192.4 0.0 copy-done.2
  192.4 1.9 fusion.10
  194.3 2.5 %pad_maximum_fusion = f32[1024,1024]{1,0:T(8,128)} fusion(f32[512,1024]{1,0:T(8,128)S(1)} %fusion.10, f32[512,1024]{1,0:T(8,128)S(1)} %bitcast.33), kind=kLoop, calls=%fused_computation.2 | loop fusion | flops 1048576 | bytes 8388608 | tf_op jit(solution)/shard_map/concatenate | solution.py:28
  196.8 0.0 reduce-scatter.2.cloned.1.call-update
  196.8 40.8 %reduce-scatter.2.cloned.1.call-done = f32[2,64,1024]{2,1,0:T(8,128)} async-done(((f32[2,512,1024]{2,1,0:T(8,128)}), f32[2,64,1024]{2,1,0:T(8,128)}) %reduce-scatter.2.cloned.1.call-update) | async-done | bytes 524304 | tf_op jit(solution)/shard_map/reduce_scatter | solution.py:29
Async XLA Ops:
  6.5 182.1 %copy-start = (f32[512,512]{1,0:T(8,128)S(1)}, f32[512,512]{1,0:T(8,128)}, u32[]{:S(2)}) copy-start(f32[512,512]{1,0:T(8,128)} %param.10) | copy-start | bytes 3145732
  12.0 155.7 %all-to-all-start = ((bf16[16,2,32,4096]{3,2,1,0:T(8,128)(2,1)}), bf16[16,2,32,4096]{3,2,1,0:T(8,128)(2,1)}, u32[]{:S(2)}, u32[]{:S(2)}) async-start(bf16[16,2,32,4096]{3,2,1,0:T(8,128)(2,1)} %stack.2), calls=%async_computation | async-start | bytes 16777216 | tf_op jit(solution)/shard_map/all_to_all | solution.py:17
  20.0 217.7 %reduce-scatter.2.cloned.1.call-start = ((), (), s32[]{:S(2)}) async-start(), calls=%async_computation.2 | async-start | bytes 4718592 | tf_op jit(solution)/shard_map/reduce_scatter | solution.py:29
  175.4 13.2 %copy-start.3 = (f32[2,64,1024]{2,1,0:T(8,128)S(1)}, f32[2,64,1024]{2,1,0:T(8,128)}, u32[]{:S(2)}) copy-start(f32[2,64,1024]{2,1,0:T(8,128)} %param.6) | copy-start | bytes 1572868
  188.5 2.0 copy-start.1
  188.7 3.8 %copy-start.2 = (f32[512,512]{1,0:T(8,128)S(1)}, f32[512,512]{1,0:T(8,128)}, u32[]{:S(2)}) copy-start(f32[512,512]{1,0:T(8,128)} %param.11) | copy-start | bytes 3145732
Sparse Core Ops, SparseCore 0:
  197.0 40.6 reduce-scatter.1
